TPU v7x, 32 devices: a whole 2x2x4 slice. The times are simulated.
32 devices in a mesh: row: 8 (over z, core), col: 4 (over y, x).
Axes of the slice: x: 2, y: 2, z: 4, core: 2. Of those that a mesh axis runs over, the one named last changes fastest.
Arguments:
- start_panel: bfloat16 [32768, 128], P(('col', 'row')), may hold values from -6 to 6
- block_values: bfloat16 [8, 4, 352, 128, 128], P('row', 'col'), may hold values from -0.078125 to 0.078125
- block_rows: int32 [8, 4, 352], P('row', 'col'), may hold values from 0 to 31, as said below
- block_cols: int32 [8, 4, 352], P('row', 'col'), may hold values from 0 to 63, as said below
- block_counts: int32 [8, 4], P('row', 'col'), may hold values from 141 to 352, as said below
Outputs:
- left_panel: bfloat16 [32768, 128], P(('row', 'col'))
- right_panel: bfloat16 [32768, 128], P(('col', 'row'))
Inputs may be any that keep to these rules, and one draw needn't show every extreme that they name: `block_rows`: block rows lie in 0 to 31 within each tile; low block rows hold more blocks; in every tile some live slot names block row 31. `block_cols`: in every tile some live slot names block column 63; a position may repeat. Only the first block_counts[r, c] slots of tile (r, c) are live; some tile fills all 352 slots.
All inputs are finite; a program needn't handle non-finite values.
Results may differ from a plain program's by a relative error of at most 0.0085.
Values may be sent and summed in bfloat16 or wider, within the bound.
No kernel may reach another device: no remote copies, remote signals or barrier semaphores. Data moves between devices by JAX's collectives and lax.ppermute only.
A program may use at most 128 MiB of HBM per device.

v0:
```python
import jax
import jax.numpy as jnp
from jax import lax
from jax.sharding import PartitionSpec as P


def tile_product(values, index_out, index_in, live_count, panel_in, out_blocks, flipped):
    block_size = values.shape[-1]
    pieces = panel_in.reshape(-1, block_size, panel_in.shape[1])
    selected = jnp.take(pieces, index_in, axis=0)
    if flipped:
        products = jnp.einsum("kij,kip->kjp", values, selected, preferred_element_type=jnp.float32)
    else:
        products = jnp.einsum("kij,kjp->kip", values, selected, preferred_element_type=jnp.float32)
    slots = jnp.arange(values.shape[0], dtype=jnp.int32)
    live = (slots < live_count).astype(jnp.float32)
    targets = jnp.arange(out_blocks, dtype=jnp.int32)
    placement = (targets[:, None] == index_out[None, :]).astype(jnp.float32) * live[None, :]
    summed = jnp.einsum("ok,kip->oip", placement, products, precision=lax.Precision.HIGHEST)
    return summed.reshape(out_blocks * block_size, panel_in.shape[1])


def gram_local(y_rounded, nodes_total):
    return jnp.dot(y_rounded.T, y_rounded, preferred_element_type=jnp.float32) / nodes_total


def apply_factor(y_rounded, gram_total):
    lower = jnp.linalg.cholesky(gram_total)
    identity = jnp.eye(gram_total.shape[0], dtype=jnp.float32)
    inverse = jax.scipy.linalg.solve_triangular(lower, identity, lower=True)
    solved = jnp.dot(y_rounded.astype(jnp.float32), inverse.T, precision=lax.Precision.HIGHEST)
    return solved.astype(jnp.bfloat16)


def global_gram(y_rounded, nodes_total):
    partial_value = gram_local(y_rounded, nodes_total)
    within = lax.psum(partial_value.astype(jnp.bfloat16), "col").astype(jnp.float32)
    return lax.psum(within, "row")


def local(start_panel, block_values, block_rows, block_cols, block_counts):
    group_rows = start_panel.shape[0]
    row_devices = lax.axis_size("row")
    col_devices = lax.axis_size("col")
    nodes_total = group_rows * row_devices * col_devices
    values = block_values[0, 0]
    rows_local = block_rows[0, 0]
    cols_local = block_cols[0, 0]
    live_count = block_counts[0, 0]
    block_size = values.shape[-1]
    row_blocks = group_rows * col_devices // block_size
    col_blocks = group_rows * row_devices // block_size
    column_tile = lax.all_gather(start_panel, "row", axis=0, tiled=True)
    left_partial = tile_product(
        values, rows_local, cols_local, live_count, column_tile, row_blocks, False
    )
    left_group = lax.psum_scatter(left_partial, "col", scatter_dimension=0, tiled=True).astype(
        jnp.bfloat16
    )
    left_panel = apply_factor(left_group, global_gram(left_group, nodes_total))
    row_tile = lax.all_gather(left_panel, "col", axis=0, tiled=True)
    right_partial = tile_product(
        values, cols_local, rows_local, live_count, row_tile, col_blocks, True
    )
    right_group = lax.psum_scatter(right_partial, "row", scatter_dimension=0, tiled=True).astype(
        jnp.bfloat16
    )
    right_panel = apply_factor(right_group, global_gram(right_group, nodes_total))
    return (left_panel, right_panel)


def solution(mesh):
    return jax.shard_map(
        local,
        mesh=mesh,
        in_specs=(
            P(("col", "row"), None),
            P("row", "col", None, None, None),
            P("row", "col", None),
            P("row", "col", None),
            P("row", "col"),
        ),
        out_specs=(P(("row", "col"), None), P(("col", "row"), None)),
        check_vma=False,
    )
```

profile of v0, /device:TPU:0, one launch (start us, length us, event | category | flops | bytes accessed | tf_op | source)
XLA Modules:
  0.0 443.7 jit_solution(17568605688700938867)
XLA Ops:
  10.7 30.8 %all-gather.3.cloned.1.call-done = bf16[8192,128]{1,0:T(8,128)(2,1)} async-done(((bf16[1024,128]{1,0:T(8,128)(2,1)}), bf16[8192,128]{1,0:T(8,128)(2,1)}) %all-gather.3.cloned.1.call-update) | async-done | bytes 2097168 | tf_op jit(solution)/shard_map/all_gather | solution.py:53
  41.5 12.6 %gather_fusion = bf16[352,128,128]{2,1,0:T(8,128)(2,1)} fusion(bf16[64,128,128]{2,1,0:T(8,128)(2,1)} %bitcast.48, s32[1024]{0:T(1024)S(1)} %pad_clamp_fusion.1), kind=kCustom, calls=%fused_computation | custom fusion | bytes 23070080 | tf_op jit(solution)/shard_map/jit(_take)/gather | solution.py:10
  54.1 21.3 %fusion.6 = f32[352,128,128]{2,1,0:T(8,128)} fusion(bf16[1,1,352,128,128]{4,3,2,1,0:T(8,128)(2,1)} %param.9, bf16[352,128,128]{2,1,0:T(8,128)(2,1)} %gather_fusion, pred[352]{0:T(512)(128)(4,1)S(1)} %compare_and_fusion.1), kind=kOutput, calls=%fused_computation.8 | convolution fusion | flops 1482162176 | bytes 46137696 | tf_op jit(solution)/shard_map/kij,kjp->kip/dot_general | solution.py:14
  75.3 23.6 %copy.17 = f32[352,128,128]{1,0,2:T(8,128)} copy(f32[352,128,128]{2,1,0:T(8,128)} %fusion.6) | data formatting | bytes 46137344 | tf_op jit(solution)/shard_map/kij,kjp->kip/dot_general | solution.py:14
  98.9 15.9 %fusion.2 = f32[32,128,128]{2,0,1:T(8,128)S(1)} fusion(f32[352,128,128]{1,0,2:T(8,128)} %copy.17, f32[352]{0:T(512)S(1)} %fusion.40, s32[352]{0:T(512)S(1)} %reduce.4), kind=kOutput, calls=%fused_computation.4 | convolution fusion | flops 2214615040 | bytes 25168640 | tf_op jit(solution)/shard_map/ok,kip->oip/dot_general | solution.py:19
  114.8 2.6 copy.11
  117.4 34.7 %reduce-scatter.3.cloned.1.call-done = f32[1024,128]{1,0:T(8,128)} async-done(((f32[4096,128]{1,0:T(8,128)}), f32[1024,128]{1,0:T(8,128)}) %reduce-scatter.3.cloned.1.call-update) | async-done | bytes 524304 | tf_op jit(solution)/shard_map/reduce_scatter | solution.py:57
  153.6 15.4 %psum.28 = bf16[128,128]{0,1:T(8,128)(2,1)S(1)} all-reduce(bf16[128,128]{0,1:T(8,128)(2,1)S(1)} %fusion.14), channel_id=1, replica_groups=mesh['row'=8,'col'=4] {'col'}, use_global_device_ids=true, to_apply=%region_1.2 | all-reduce | flops 16384 | bytes 65536 | tf_op jit(solution)/shard_map/psum | solution.py:37
  169.0 26.8 %all-reduce.2 = f32[128,128]{0,1:T(8,128)S(1)} all-reduce(bf16[128,128]{0,1:T(8,128)(2,1)S(1)} %psum.28), channel_id=1, replica_groups=mesh['row'=8,'col'=4] {'row'}, use_global_device_ids=true, to_apply=%region_2.3 | all-reduce | flops 16384 | bytes 98304 | tf_op jit(solution)/shard_map/psum | solution.py:38
  195.9 11.7 %cholesky.44 = f32[128,128]{1,0:T(8,128)S(1)} custom-call(f32[128,128]{1,0:T(8,128)S(1)} %fusion.31), custom_call_target="Cholesky" | custom-call | tf_op jit(solution)/shard_map/jit(cholesky)/cholesky | solution.py:28
  209.0 9.8 %custom-call.6 = f32[1,128,128]{1,2,0:T(8,128)S(1)} custom-call(f32[1,128,128]{2,1,0:T(8,128)S(1)} %fusion.26), custom_call_target="InvertDiagBlocksLowerTriangular" | custom-call | tf_op jit(solution)/shard_map/jit(_solve_triangular)/triangular_solve | solution.py:30
  219.1 2.1 convolution_convert_fusion.1
  221.5 23.5 %all-gather.5.cloned.1.call-done = bf16[4096,128]{1,0:T(8,128)(2,1)} async-done(((bf16[1024,128]{1,0:T(8,128)(2,1)}), bf16[4096,128]{1,0:T(8,128)(2,1)}) %all-gather.5.cloned.1.call-update) | async-done | bytes 1048592 | tf_op jit(solution)/shard_map/all_gather | solution.py:61
  245.0 12.2 %gather_fusion.1 = bf16[352,128,128]{2,1,0:T(8,128)(2,1)} fusion(bf16[32,128,128]{2,1,0:T(8,128)(2,1)} %bitcast.47, s32[1024]{0:T(1024)S(1)} %pad_clamp_fusion), kind=kCustom, calls=%fused_computation.1 | custom fusion | bytes 23070080 | tf_op jit(solution)/shard_map/jit(_take)/gather | solution.py:10
  257.2 14.6 %fusion.4 = f32[352,128,128]{2,1,0:T(8,128)} fusion(bf16[1,1,352,128,128]{4,3,2,1,0:T(8,128)(2,1)} %param.9, bf16[352,128,128]{2,1,0:T(8,128)(2,1)} %gather_fusion.1, pred[352]{0:T(512)(128)(4,1)S(1)} %compare_and_fusion), kind=kOutput, calls=%fused_computation.6 | convolution fusion | flops 1482162176 | bytes 46137696 | tf_op jit(solution)/shard_map/kij,kip->kjp/dot_general | solution.py:12
  271.8 23.6 %copy.19 = f32[352,128,128]{1,0,2:T(8,128)} copy(f32[352,128,128]{2,1,0:T(8,128)} %fusion.4) | data formatting | bytes 46137344 | tf_op jit(solution)/shard_map/kij,kip->kjp/dot_general | solution.py:12
  295.3 17.3 %fusion = f32[64,128,128]{2,0,1:T(8,128)S(1)} fusion(f32[352,128,128]{1,0,2:T(8,128)} %copy.19, f32[352]{0:T(512)S(1)} %fusion.40, s32[352]{0:T(512)S(1)} %reduce.5), kind=kOutput, calls=%fused_computation.2 | convolution fusion | flops 4429230080 | bytes 27265792 | tf_op jit(solution)/shard_map/ok,kip->oip/dot_general | solution.py:19
  312.7 4.4 copy.14
  317.0 50.1 %reduce-scatter.5.cloned.1.call-done = f32[1024,128]{1,0:T(8,128)} async-done(((f32[8192,128]{1,0:T(8,128)}), f32[1024,128]{1,0:T(8,128)}) %reduce-scatter.5.cloned.1.call-update) | async-done | bytes 524304 | tf_op jit(solution)/shard_map/reduce_scatter | solution.py:65
  368.6 16.5 %psum.30 = bf16[128,128]{0,1:T(8,128)(2,1)S(1)} all-reduce(bf16[128,128]{0,1:T(8,128)(2,1)S(1)} %fusion.15), channel_id=1, replica_groups=mesh['row'=8,'col'=4] {'col'}, use_global_device_ids=true, to_apply=%region_6.9 | all-reduce | flops 16384 | bytes 65536 | tf_op jit(solution)/shard_map/psum | solution.py:37
  385.1 26.4 %all-reduce.3 = f32[128,128]{0,1:T(8,128)S(1)} all-reduce(bf16[128,128]{0,1:T(8,128)(2,1)S(1)} %psum.30), channel_id=1, replica_groups=mesh['row'=8,'col'=4] {'row'}, use_global_device_ids=true, to_apply=%region_7.10 | all-reduce | flops 16384 | bytes 98304 | tf_op jit(solution)/shard_map/psum | solution.py:38
  411.6 11.7 %cholesky.55 = f32[128,128]{1,0:T(8,128)S(1)} custom-call(f32[128,128]{1,0:T(8,128)S(1)} %fusion.29), custom_call_target="Cholesky" | custom-call | tf_op jit(solution)/shard_map/jit(cholesky)/cholesky | solution.py:28
  424.7 9.8 %custom-call.7 = f32[1,128,128]{1,2,0:T(8,128)S(1)} custom-call(f32[1,128,128]{2,1,0:T(8,128)S(1)} %fusion.27), custom_call_target="InvertDiagBlocksLowerTriangular" | custom-call | tf_op jit(solution)/shard_map/jit(_solve_triangular)/triangular_solve | solution.py:30
  434.8 2.1 convolution_convert_fusion
  (33 shorter events, 9.6 us)
Async XLA Ops:
  7.2 34.3 %all-gather.3.cloned.1.call-start = ((), (), s32[]{:S(2)}) async-start(), calls=%async_computation.2 | async-start | bytes 2359296 | tf_op jit(solution)/shard_map/all_gather | solution.py:53
  7.9 144.2 %reduce-scatter.3.cloned.1.call-start = ((), (), s32[]{:S(2)}) async-start(), calls=%async_computation.3 | async-start | bytes 2621440 | tf_op jit(solution)/shard_map/reduce_scatter | solution.py:57
  98.9 122.5 %copy-start = (s32[1,1,352]{2,1,0:T(1,128)S(1)}, s32[1,1,352]{2,1,0:T(1,128)}, u32[]{:S(2)}) copy-start(s32[1,1,352]{2,1,0:T(1,128)} %param.10) | copy-start | bytes 4228
  117.3 127.7 %all-gather.5.cloned.1.call-start = ((), (), s32[]{:S(2)}) async-start(), calls=%async_computation.4 | async-start | bytes 1310720 | tf_op jit(solution)/shard_map/all_gather | solution.py:61
  221.2 145.9 %reduce-scatter.5.cloned.1.call-start = ((), (), s32[]{:S(2)}) async-start(), calls=%async_computation.5 | async-start | bytes 4718592 | tf_op jit(solution)/shard_map/reduce_scatter | solution.py:65
Sparse Core Ops, SparseCore 0:
  9.6 31.8 all-gather.2
  117.5 34.5 reduce-scatter.2
  221.3 23.6 all-gather.4
  317.2 49.9 reduce-scatter.4
where the time goes:
time: 452 us; the launch traced here: 444 us
  waiting for transfers between devices  140 us (31%)
  blocking collectives  85.1 us (19%)
  local copies, waits for them, and re-layouts  79 us (17%)
  matrix products  76.8 us (17%)
  other arithmetic  47.9 us (11%)
  between operations  14.8 us (3%)
    psum x2, blocking collectives, global_gram(): return lax.psum(within, 'row')  53.1 us
    reduce_scatter x1, waiting for transfers between devices, local(): lax.psum_scatter(right_partial, 'row', scatter_dimension=0, tiled=True)  50.1 us
    reduce_scatter x1, waiting for transfers between devices, local(): lax.psum_scatter(left_partial, 'col', scatter_dimension=0, tiled=True)  34.7 us
    dot_general x2, matrix products, tile_product(): jnp.einsum('ok,kip->oip', placement, products, precision=lax.Precision.HI...  33.2 us
    psum x2, blocking collectives, global_gram(): lax.psum(partial_value.astype(jnp.bfloat16), 'col').astype(jnp.float32)  31.9 us
    all_gather x1, waiting for transfers between devices, local(): column_tile = lax.all_gather(start_panel, 'row', axis=0, tiled=True)  30.8 us
    another operation x6, other arithmetic, apply_factor(): lower = jnp.linalg.cholesky(gram_total)  24.8 us
    gather x2, local copies, waits for them, and re-layouts, tile_product(): selected = jnp.take(pieces, index_in, axis=0)  24.8 us
  transfers between devices with their start and end apart: 4, of which 4 were waited for; matrix products, arithmetic and copies ran while one was open for 0% of the time, Pallas kernels for 0%

commit v1 on v0

--- a/solution.py
+++ b/solution.py
@@ -34,7 +34,9 @@
 
 def global_gram(y_rounded, nodes_total):
     partial_value = gram_local(y_rounded, nodes_total)
-    within = lax.psum(partial_value.astype(jnp.bfloat16), "col").astype(jnp.float32)
+    within = jnp.sum(lax.all_gather(partial_value.astype(jnp.bfloat16), "col"), axis=0).astype(
+        jnp.float32
+    )
     return lax.psum(within, "row")
 
 

time: 452 us -> 438 us (0.969)
  blocking collectives: 85.1 us -> 70.7 us
    psum x2 -> x0, blocking collectives: 31.9 us -> none  [global_gram(): lax.psum(partial_value.astype(jnp.bfloat16), 'col').astype(jnp.float32)]
    all_gather x0 -> x2, blocking collectives: none -> 16.9 us  [global_gram(): lax.all_gather(partial_value.astype(jnp.bfloat16), 'col')]
  transfers between devices with their start and end apart: 4 -> 4, of which waited for: 4 -> 4; matrix products, arithmetic and copies ran while one was open for 0% -> 1% of each run, Pallas kernels for 0% -> 0%
where the time goes in v1:
time: 438 us; the launch traced here: 430 us
  waiting for transfers between devices  140 us (32%)
  local copies, waits for them, and re-layouts  79.2 us (18%)
  matrix products  76.8 us (18%)
  blocking collectives  70.7 us (16%)
  other arithmetic  47.9 us (11%)
  between operations  14.8 us (3%)
    psum x2, blocking collectives, global_gram(): return lax.psum(within, 'row')  53.8 us
    reduce_scatter x1, waiting for transfers between devices, local(): lax.psum_scatter(right_partial, 'row', scatter_dimension=0, tiled=True)  50.1 us
    reduce_scatter x1, waiting for transfers between devices, local(): lax.psum_scatter(left_partial, 'col', scatter_dimension=0, tiled=True)  34.7 us
    dot_general x2, matrix products, tile_product(): jnp.einsum('ok,kip->oip', placement, products, precision=lax.Precision.HI...  33.2 us
    all_gather x1, waiting for transfers between devices, local(): column_tile = lax.all_gather(start_panel, 'row', axis=0, tiled=True)  30.8 us
    another operation x6, other arithmetic, apply_factor(): lower = jnp.linalg.cholesky(gram_total)  24.8 us
    gather x2, local copies, waits for them, and re-layouts, tile_product(): selected = jnp.take(pieces, index_in, axis=0)  24.8 us
    all_gather x1, waiting for transfers between devices, local(): row_tile = lax.all_gather(left_panel, 'col', axis=0, tiled=True)  23.6 us
  transfers between devices with their start and end apart: 4, of which 4 were waited for; matrix products, arithmetic and copies ran while one was open for 1% of the time, Pallas kernels for 0%

profile of v1, /device:TPU:0, one launch (start us, length us, event | category | flops | bytes accessed | tf_op | source)
XLA Modules:
  0.0 429.6 jit_solution(16980808959628491625)
XLA Ops:
  10.7 30.8 %all-gather.5.cloned.1.call-done = bf16[8192,128]{1,0:T(8,128)(2,1)} async-done(((bf16[1024,128]{1,0:T(8,128)(2,1)}), bf16[8192,128]{1,0:T(8,128)(2,1)}) %all-gather.5.cloned.1.call-update) | async-done | bytes 2097168 | tf_op jit(solution)/shard_map/all_gather | solution.py:55
  41.5 12.6 %gather_fusion = bf16[352,128,128]{2,1,0:T(8,128)(2,1)} fusion(bf16[64,128,128]{2,1,0:T(8,128)(2,1)} %bitcast.54, s32[1024]{0:T(1024)S(1)} %pad_clamp_fusion.1), kind=kCustom, calls=%fused_computation | custom fusion | bytes 23070080 | tf_op jit(solution)/shard_map/jit(_take)/gather | solution.py:10
  54.1 21.3 %fusion.8 = f32[352,128,128]{1,2,0:T(8,128)} fusion(bf16[1,1,352,128,128]{4,3,2,1,0:T(8,128)(2,1)} %param.9, bf16[352,128,128]{2,1,0:T(8,128)(2,1)} %gather_fusion, pred[352]{0:T(512)(128)(4,1)S(1)} %compare_and_fusion.1), kind=kOutput, calls=%fused_computation.10 | convolution fusion | flops 1482162176 | bytes 46137696 | tf_op jit(solution)/shard_map/kij,kjp->kip/dot_general | solution.py:14
  75.3 23.6 %copy.22 = f32[352,128,128]{2,0,1:T(8,128)} copy(f32[352,128,128]{1,2,0:T(8,128)} %fusion.8) | data formatting | bytes 46137344 | tf_op jit(solution)/shard_map/kij,kjp->kip/dot_general | solution.py:14
  98.9 15.9 %fusion.39 = f32[32,128,128]{2,0,1:T(8,128)S(1)} fusion(f32[352,128,128]{2,0,1:T(8,128)} %copy.22, f32[352]{0:T(512)S(1)} %fusion.48, s32[352]{0:T(512)S(1)} %reduce.6), kind=kOutput, calls=%fused_computation.46 | convolution fusion | flops 2214615040 | bytes 25168640 | tf_op jit(solution)/shard_map/ok,kip->oip/dot_general | solution.py:19
  114.8 2.6 copy.23
  117.4 34.7 %reduce-scatter.3.cloned.1.call-done = f32[1024,128]{1,0:T(8,128)} async-done(((f32[4096,128]{1,0:T(8,128)}), f32[1024,128]{1,0:T(8,128)}) %reduce-scatter.3.cloned.1.call-update) | async-done | bytes 524304 | tf_op jit(solution)/shard_map/reduce_scatter | solution.py:59
  153.6 8.5 %all-gather = bf16[512,128]{1,0:T(8,128)(2,1)S(1)} all-gather(bf16[128,128]{1,0:T(8,128)(2,1)S(1)} %fusion.20), channel_id=2, replica_groups=mesh['row'=8,'col'=4] {'col'}, dimensions={0}, use_global_device_ids=true | all-gather | bytes 163840 | tf_op jit(solution)/shard_map/all_gather | solution.py:37
  162.2 27.2 %all-reduce.2 = f32[128,128]{0,1:T(8,128)S(1)} all-reduce(bf16[128,128]{0,1:T(8,128)(2,1)S(1)} %copy.24), channel_id=1, replica_groups=mesh['row'=8,'col'=4] {'row'}, use_global_device_ids=true, to_apply=%region_2.3 | all-reduce | flops 16384 | bytes 98304 | tf_op jit(solution)/shard_map/psum | solution.py:40
  189.5 11.7 %cholesky.44 = f32[128,128]{1,0:T(8,128)S(1)} custom-call(f32[128,128]{1,0:T(8,128)S(1)} %fusion.38), custom_call_target="Cholesky" | custom-call | tf_op jit(solution)/shard_map/jit(cholesky)/cholesky | solution.py:28
  202.6 9.8 %custom-call.6 = f32[1,128,128]{1,2,0:T(8,128)S(1)} custom-call(f32[1,128,128]{2,1,0:T(8,128)S(1)} %fusion.33), custom_call_target="InvertDiagBlocksLowerTriangular" | custom-call | tf_op jit(solution)/shard_map/jit(_solve_triangular)/triangular_solve | solution.py:30
  212.7 2.1 convolution_convert_fusion.1
  215.1 23.6 %all-gather.7.cloned.1.call-done = bf16[4096,128]{1,0:T(8,128)(2,1)} async-done(((bf16[1024,128]{1,0:T(8,128)(2,1)}), bf16[4096,128]{1,0:T(8,128)(2,1)}) %all-gather.7.cloned.1.call-update) | async-done | bytes 1048592 | tf_op jit(solution)/shard_map/all_gather | solution.py:63
  238.7 12.2 %gather_fusion.1 = bf16[352,128,128]{2,1,0:T(8,128)(2,1)} fusion(bf16[32,128,128]{2,1,0:T(8,128)(2,1)} %bitcast.53, s32[1024]{0:T(1024)S(1)} %pad_clamp_fusion), kind=kCustom, calls=%fused_computation.1 | custom fusion | bytes 23070080 | tf_op jit(solution)/shard_map/jit(_take)/gather | solution.py:10
  250.9 14.6 %fusion.13 = f32[352,128,128]{1,2,0:T(8,128)} fusion(bf16[1,1,352,128,128]{4,3,2,1,0:T(8,128)(2,1)} %param.9, bf16[352,128,128]{2,1,0:T(8,128)(2,1)} %gather_fusion.1, pred[352]{0:T(512)(128)(4,1)S(1)} %compare_and_fusion), kind=kOutput, calls=%fused_computation.11 | convolution fusion | flops 1482162176 | bytes 46137696 | tf_op jit(solution)/shard_map/kij,kip->kjp/dot_general | solution.py:12
  265.5 23.6 %copy.27 = f32[352,128,128]{2,0,1:T(8,128)} copy(f32[352,128,128]{1,2,0:T(8,128)} %fusion.13) | data formatting | bytes 46137344 | tf_op jit(solution)/shard_map/kij,kip->kjp/dot_general | solution.py:12
  289.1 17.3 %fusion.26 = f32[64,128,128]{2,0,1:T(8,128)S(1)} fusion(f32[352,128,128]{2,0,1:T(8,128)} %copy.27, f32[352]{0:T(512)S(1)} %fusion.48, s32[352]{0:T(512)S(1)} %reduce.7), kind=kOutput, calls=%fused_computation.24 | convolution fusion | flops 4429230080 | bytes 27265792 | tf_op jit(solution)/shard_map/ok,kip->oip/dot_general | solution.py:19
  306.4 4.4 %copy.28 = f32[64,128,128]{2,1,0:T(8,128)} copy(f32[64,128,128]{2,0,1:T(8,128)S(1)} %fusion.26) | data formatting | bytes 8388608 | tf_op jit(solution)/shard_map/ok,kip->oip/dot_general | solution.py:19
  310.8 50.1 %reduce-scatter.5.cloned.1.call-done = f32[1024,128]{1,0:T(8,128)} async-done(((f32[8192,128]{1,0:T(8,128)}), f32[1024,128]{1,0:T(8,128)}) %reduce-scatter.5.cloned.1.call-update) | async-done | bytes 524304 | tf_op jit(solution)/shard_map/reduce_scatter | solution.py:67
  362.3 8.4 %all-gather.1 = bf16[512,128]{1,0:T(8,128)(2,1)S(1)} all-gather(bf16[128,128]{1,0:T(8,128)(2,1)S(1)} %fusion.21), channel_id=3, replica_groups=mesh['row'=8,'col'=4] {'col'}, dimensions={0}, use_global_device_ids=true | all-gather | bytes 163840 | tf_op jit(solution)/shard_map/all_gather | solution.py:37
  370.9 26.6 %all-reduce.3 = f32[128,128]{0,1:T(8,128)S(1)} all-reduce(bf16[128,128]{0,1:T(8,128)(2,1)S(1)} %copy.29), channel_id=1, replica_groups=mesh['row'=8,'col'=4] {'row'}, use_global_device_ids=true, to_apply=%region_7.10 | all-reduce | flops 16384 | bytes 98304 | tf_op jit(solution)/shard_map/psum | solution.py:40
  397.6 11.7 %cholesky.55 = f32[128,128]{1,0:T(8,128)S(1)} custom-call(f32[128,128]{1,0:T(8,128)S(1)} %fusion.36), custom_call_target="Cholesky" | custom-call | tf_op jit(solution)/shard_map/jit(cholesky)/cholesky | solution.py:28
  410.7 9.8 %custom-call.7 = f32[1,128,128]{1,2,0:T(8,128)S(1)} custom-call(f32[1,128,128]{2,1,0:T(8,128)S(1)} %fusion.34), custom_call_target="InvertDiagBlocksLowerTriangular" | custom-call | tf_op jit(solution)/shard_map/jit(_solve_triangular)/triangular_solve | solution.py:30
  420.8 2.1 convolution_convert_fusion
  (37 shorter events, 9.9 us)
Async XLA Ops:
  7.2 34.3 %all-gather.5.cloned.1.call-start = ((), (), s32[]{:S(2)}) async-start(), calls=%async_computation.2 | async-start | bytes 2359296 | tf_op jit(solution)/shard_map/all_gather | solution.py:55
  7.9 144.2 %reduce-scatter.3.cloned.1.call-start = ((), (), s32[]{:S(2)}) async-start(), calls=%async_computation.3 | async-start | bytes 2621440 | tf_op jit(solution)/shard_map/reduce_scatter | solution.py:59
  98.9 116.2 %copy-start = (s32[1,1,352]{2,1,0:T(1,128)S(1)}, s32[1,1,352]{2,1,0:T(1,128)}, u32[]{:S(2)}) copy-start(s32[1,1,352]{2,1,0:T(1,128)} %param.10) | copy-start | bytes 4228
  117.3 121.4 %all-gather.7.cloned.1.call-start = ((), (), s32[]{:S(2)}) async-start(), calls=%async_computation.4 | async-start | bytes 1310720 | tf_op jit(solution)/shard_map/all_gather | solution.py:63
  214.9 146.0 %reduce-scatter.5.cloned.1.call-start = ((), (), s32[]{:S(2)}) async-start(), calls=%async_computation.5 | async-start | bytes 4718592 | tf_op jit(solution)/shard_map/reduce_scatter | solution.py:67
Sparse Core Ops, SparseCore 0:
  9.6 31.8 all-gather.4
  117.5 34.5 reduce-scatter.2
  215.0 23.7 all-gather.6
  310.9 49.9 reduce-scatter.4
